TPU v7x, 32 devices: a whole 2x2x4 slice. The times are simulated.
32 devices in a mesh: seq: 16 (over z, y, x), head: 2 (over core).
Axes of the slice: x: 2, y: 2, z: 4, core: 2. Of those that a mesh axis runs over, the one named last changes fastest.
Arguments:
- queries: bfloat16 [12288, 128], P('seq'), may hold values from -6 to 6
- keys: bfloat16 [12288, 128], P('seq'), may hold values from -0.023925781 to 0.023925781
- values: bfloat16 [12288, 8192], P('seq', 'head'), may hold values from -6 to 6
- log_decay: float32 [128, 12288], P('head', 'seq'), may hold values from -0.8 to 0
- level_weight: bfloat16 [5, 128, 12288], P(None, 'head', 'seq'), may hold values from 0.099609375 to 1
- skip: float32 [128], P('head'), may hold values from 0.4 to 4.5
- norm_gain: bfloat16 [8192], P('head'), may hold values from 0.25 to 1.75
Outputs:
- normed: bfloat16 [12288, 8192], P('seq', 'head')
All inputs are finite; a program needn't handle non-finite values.
Results may differ from a plain program's by a relative error of at most 0.007.
Values sent between devices are 32-bit elements; how exact they have to be, the bound alone decides.
No kernel may reach another device: no remote copies, remote signals or barrier semaphores. Data moves between devices by JAX's collectives and lax.ppermute only.
A program may use at most 192 MiB of HBM per device.

v0:
```python
import jax
import jax.numpy as jnp
from jax import lax
from jax.sharding import PartitionSpec as P


def partner(value, axis, stride):
    return lax.ppermute(value, axis, [(i, i ^ 1 << stride) for i in range(lax.axis_size(axis))])


def split_project(queries, state):
    upper_part = state.astype(jnp.bfloat16)
    lower_part = (state - upper_part.astype(jnp.float32)).astype(jnp.bfloat16)
    first = jnp.einsum("tn,hnp->htp", queries, upper_part, preferred_element_type=jnp.float32)
    second = jnp.einsum("tn,hnp->htp", queries, lower_part, preferred_element_type=jnp.float32)
    return first + second


def shards(queries, keys, values, log_decay, level_weight, skip, norm_gain):
    tok_rows = queries.shape[0]
    head_count = log_decay.shape[0]
    chan_width = values.shape[1]
    head_size = chan_width // head_count
    decay_cum = jnp.cumsum(log_decay, axis=1)
    block_totals = decay_cum[:, -1]
    scores = jnp.dot(queries, keys.T, preferred_element_type=jnp.float32)
    position = jnp.arange(tok_rows, dtype=jnp.int32)
    causal = position[:, None] >= position[None, :]
    head_values = values.reshape(tok_rows, head_count, head_size).transpose(1, 0, 2)
    keys_f32 = keys.astype(jnp.float32)

    def head_terms(inputs):
        cum_head, head_vals = inputs
        spread_in = jnp.where(causal, cum_head[:, None] - cum_head[None, :], 0.0)
        mixing = (jnp.where(causal, jnp.exp(spread_in), 0.0) * scores).astype(jnp.bfloat16)
        inner = jnp.dot(mixing, head_vals, preferred_element_type=jnp.float32)
        scaled_keys = (keys_f32 * jnp.exp(cum_head[-1] - cum_head)[:, None]).astype(jnp.bfloat16)
        head_state = jnp.einsum(
            "sn,sp->np", scaled_keys, head_vals, preferred_element_type=jnp.float32
        )
        return (inner, head_state)

    inner_all, states = lax.map(head_terms, (decay_cum, head_values))
    weights_f32 = level_weight.astype(jnp.float32)
    mixed_out = weights_f32[0][:, :, None] * inner_all + skip[:, None, None] * head_values.astype(
        jnp.float32
    )
    level_count = lax.axis_size("seq").bit_length() - 1
    seq_index = lax.axis_index("seq")
    group_state = states
    group_total = block_totals
    offset = jnp.zeros_like(block_totals)
    for level_no in range(level_count):
        level_bit = seq_index // (1 << level_no) % 2
        level_flag = level_bit.astype(jnp.float32)
        partner_state, partner_total = partner((group_state, group_total), "seq", level_no)
        level_coef = weights_f32[level_no + 1] * level_flag * jnp.exp(decay_cum + offset[:, None])
        projected = split_project(queries, partner_state)
        mixed_out = mixed_out + level_coef[:, :, None] * projected
        if level_no + 1 < level_count:
            left_state = jnp.where(level_bit == 1, partner_state, group_state)
            right_state = jnp.where(level_bit == 1, group_state, partner_state)
            right_total = jnp.where(level_bit == 1, group_total, partner_total)
            group_state = jnp.exp(right_total)[:, None, None] * left_state + right_state
        offset = offset + level_flag * partner_total
        group_total = group_total + partner_total
    local_squares = jnp.sum(mixed_out * mixed_out, axis=(0, 2))
    sum_squares = lax.psum(local_squares, "head")
    inv_rms = lax.rsqrt(sum_squares / (head_count * head_size * lax.axis_size("head")) + 1e-05)
    scaled_out = mixed_out * inv_rms[None, :, None]
    result_rows = scaled_out.transpose(1, 0, 2).reshape(tok_rows, chan_width) * norm_gain.astype(
        jnp.float32
    )
    return result_rows.astype(jnp.bfloat16)


def solution(mesh):
    placed = (
        P("seq", None),
        P("seq", None),
        P("seq", "head"),
        P("head", "seq"),
        P(None, "head", "seq"),
        P("head"),
        P("head"),
    )
    return jax.shard_map(
        shards, mesh=mesh, in_specs=placed, out_specs=P("seq", "head"), check_vma=False
    )
```

profile of v0, /device:TPU:25, one launch (start us, length us, event | category | flops | bytes accessed | tf_op | source)
XLA Modules:
  0.0 685.5 jit_solution(8669186437602289343)
XLA Ops:
  5.5 8.6 %copy.14 = bf16[768,4096]{0,1:T(8,128)(2,1)} copy(bf16[768,4096]{1,0:T(8,128)(2,1)} %param.11) | data formatting | bytes 12582912 | tf_op args[2]
  14.2 336.3 %while.14 = (s32[]{:T(128)}, f32[64,768,64]{1,2,0:T(8,128)}, f32[64,128,64]{1,2,0:T(8,128)}, f32[64,768]{1,0:T(8,128)S(1)}, f32[768,768]{1,0:T(8,128)S(1)}, /*in...) while((s32[]{:T(128)}, f32[64,768,64]{1,2,0:T(8,128)}, ...), condition=%wide.region_3.4_spmd.clone.clone, body=%wide.region_2.3_spmd.clone.clone.sunk | while | flops 91816704 | bytes 3204237 | solution.py:43
  27.7 2.2 fusion.72
  33.0 2.2 fusion.72
  38.2 2.2 fusion.72
  59.2 2.2 fusion.72
  75.0 2.2 fusion.72
  96.0 2.2 fusion.72
  106.5 2.2 fusion.72
  117.0 2.2 fusion.72
  122.3 2.2 fusion.72
  127.5 2.2 fusion.72
  132.8 2.2 fusion.72
  143.3 2.2 fusion.72
  148.6 2.2 fusion.72
  164.3 2.2 fusion.72
  185.4 2.2 fusion.72
  190.6 2.2 fusion.72
  201.1 2.2 fusion.72
  206.4 2.2 fusion.72
  237.9 2.2 fusion.72
  253.7 2.2 fusion.72
  258.9 2.2 fusion.72
  274.7 2.2 fusion.72
  285.2 2.2 fusion.72
  290.5 2.2 fusion.72
  295.8 2.2 fusion.72
  311.5 2.2 fusion.72
  322.0 2.2 fusion.72
  352.2 45.0 %collective-permute-done.1 = f32[64]{0:T(128)S(1)} collective-permute-done((f32[64]{0:T(128)S(1)}, f32[64]{0:T(128)S(1)}, u32[]{:S(2)}, u32[]{:S(2)}) %collective-permute-start.1) | collective-permute-done | bytes 288 | tf_op jit(solution)/shard_map/ppermute | solution.py:8
  397.2 3.3 select_add_fusion.2
  402.0 44.4 %collective-permute-done.3 = f32[64]{0:T(128)S(1)} collective-permute-done((f32[64]{0:T(128)S(1)}, f32[64]{0:T(128)S(1)}, u32[]{:S(2)}, u32[]{:S(2)}) %collective-permute-start.3) | collective-permute-done | bytes 288 | tf_op jit(solution)/shard_map/ppermute | solution.py:8
  446.4 3.9 select_add_fusion.1
  453.7 41.7 %collective-permute-done.5 = f32[64]{0:T(128)S(1)} collective-permute-done((f32[64]{0:T(128)S(1)}, f32[64]{0:T(128)S(1)}, u32[]{:S(2)}, u32[]{:S(2)}) %collective-permute-start.5) | collective-permute-done | bytes 288 | tf_op jit(solution)/shard_map/ppermute | solution.py:8
  496.5 6.3 fusion.24
  502.8 6.4 fusion.37
  509.1 2.6 select_add_fusion
  511.9 8.5 %fusion.25 = f32[64,64,768]{2,1,0:T(8,128)} fusion(f32[64,128,64]{1,2,0:T(8,128)} %collective-permute-done.2, bf16[768,128]{1,0:T(8,128)(2,1)S(1)} %copy-done), kind=kOutput, calls=%fused_computation.38 | convolution fusion | flops 807403520 | bytes 14876672 | tf_op jit(solution)/shard_map/tn,hnp->htp/dot_general | solution.py:15
  520.4 8.0 %fusion.34 = f32[64,64,768]{2,1,0:T(8,128)} fusion(f32[64,128,64]{1,2,0:T(8,128)} %collective-permute-done.2, bf16[768,128]{1,0:T(8,128)(2,1)S(1)} %copy-done), kind=kOutput, calls=%fused_computation.47 | convolution fusion | flops 805830656 | bytes 14876672 | tf_op jit(solution)/shard_map/tn,hnp->htp/dot_general | solution.py:14
  528.3 8.5 %fusion.26 = f32[64,64,768]{2,1,0:T(8,128)} fusion(f32[64,128,64]{1,2,0:T(8,128)} %collective-permute-done.4, bf16[768,128]{1,0:T(8,128)(2,1)S(1)} %copy-done), kind=kOutput, calls=%fused_computation.39 | convolution fusion | flops 807403520 | bytes 14876672 | tf_op jit(solution)/shard_map/tn,hnp->htp/dot_general | solution.py:15
  536.8 7.9 %fusion.31 = f32[64,64,768]{2,1,0:T(8,128)} fusion(f32[64,128,64]{1,2,0:T(8,128)} %collective-permute-done.4, bf16[768,128]{1,0:T(8,128)(2,1)S(1)} %copy-done), kind=kOutput, calls=%fused_computation.44 | convolution fusion | flops 805830656 | bytes 14876672 | tf_op jit(solution)/shard_map/tn,hnp->htp/dot_general | solution.py:14
  544.7 60.4 %collective-permute-done.6 = f32[64,128,64]{1,2,0:T(8,128)S(1)} collective-permute-done((f32[64,128,64]{1,2,0:T(8,128)S(1)}, f32[64,128,64]{1,2,0:T(8,128)S(1)}, u32[]{:S(2)}, u32[]{:S(2)}) %collective-permute-start.6) | collective-permute-done | bytes 2097184 | tf_op jit(solution)/shard_map/ppermute | solution.py:8
  605.1 6.5 fusion.27
  611.7 38.9 %multiply_reduce_fusion = (f32[768]{0:T(1024)S(1)}, f32[64,768,64]{1,2,0:T(8,128)}) fusion(f32[64,64,768]{2,1,0:T(8,128)} %fusion.27, bf16[768,128]{1,0:T(8,128)(2,1)S(1)} %copy-done, f32[64,128,64]{1,2,0:T(8,128)S(1)} %collective-permute-done.6, f32[64,768]{1,0:T(8,128)S(1)} %copy-done.4, f32[64,64,768]{2,1,0:T(8,128)} %fusion.31, ...), kind=kOutput, calls=%fused_computation.28 | convolution fusion | flops 862452992 | bytes 122817792 | tf_op jit(solution)/shard_map/tn,hnp->htp/dot_general | solution.py:14
  650.6 2.6 psum.7
  653.2 10.8 %broadcast_multiply_fusion = f32[64,768,64]{1,2,0:T(8,128)} fusion(f32[64,768,64]{1,2,0:T(8,128)} %get-tuple-element.130, f32[768]{0:T(1024)S(1)} %add_rsqrt_fusion), kind=kLoop, calls=%fused_computation.29 | loop fusion | flops 3145728 | bytes 25168896 | tf_op jit(solution)/shard_map/mul | solution.py:70
  664.0 12.6 %copy.16 = f32[768,4096]{1,0:T(8,128)} copy(f32[768,4096]{0,1:T(8,128)} %bitcast.105) | data formatting | bytes 25165824 | tf_op jit(solution)/shard_map/reshape | solution.py:71
  676.6 9.0 %multiply_convert_fusion.2 = bf16[768,4096]{1,0:T(8,128)(2,1)} fusion(f32[768,4096]{1,0:T(8,128)} %copy.16, f32[4096]{0:T(1024)S(1)} %convert_element_type.88), kind=kLoop, calls=%fused_computation.27 | loop fusion | flops 6291456 | bytes 18890752 | tf_op jit(solution)/shard_map/convert_element_type | solution.py:74
  (339 shorter events, 289.0 us)
Async XLA Ops:
  0.0 4.1 copy-start
  350.5 46.7 %collective-permute-start = (f32[64,128,64]{1,2,0:T(8,128)}, f32[64,128,64]{1,2,0:T(8,128)S(1)}, u32[]{:S(2)}, u32[]{:S(2)}) collective-permute-start(f32[64,128,64]{1,2,0:T(8,128)} %get-tuple-element.52), channel_id=1, source_target_pairs={{0,2},{2,0},{4,6},{6,4},{8,10},{10,8},{12,14},{14,12},{16,18},{18,... | collective-permute-start | bytes 6291464 | tf_op jit(solution)/shard_map/ppermute | solution.py:8
  351.9 45.3 %collective-permute-start.1 = (f32[64]{0:T(128)S(1)}, f32[64]{0:T(128)S(1)}, u32[]{:S(2)}, u32[]{:S(2)}) collective-permute-start(f32[64]{0:T(128)S(1)} %slice_reduce_fusion.1), channel_id=1, source_target_pairs={{0,2},{2,0},{4,6},{6,4},{8,10},{10,8},{12,14},{14,12},{16,18},{18,... | collective-permute-start | bytes 776 | tf_op jit(solution)/shard_map/ppermute | solution.py:8
  400.5 45.9 %collective-permute-start.2 = (f32[64,128,64]{1,2,0:T(8,128)}, f32[64,128,64]{1,2,0:T(8,128)}, u32[]{:S(2)}, u32[]{:S(2)}) collective-permute-start(f32[64,128,64]{1,2,0:T(8,128)} %select_add_fusion.2), channel_id=1, source_target_pairs={{0,4},{2,6},{4,0},{6,2},{8,12},{10,14},{12,8},{14,10},{16,20},{18,... | collective-permute-start | bytes 6291464 | tf_op jit(solution)/shard_map/ppermute | solution.py:8
  401.8 44.6 %collective-permute-start.3 = (f32[64]{0:T(128)S(1)}, f32[64]{0:T(128)S(1)}, u32[]{:S(2)}, u32[]{:S(2)}) collective-permute-start(f32[64]{0:T(128)S(1)} %get-tuple-element.126), channel_id=1, source_target_pairs={{0,4},{2,6},{4,0},{6,2},{8,12},{10,14},{12,8},{14,10},{16,20},{18,... | collective-permute-start | bytes 776 | tf_op jit(solution)/shard_map/ppermute | solution.py:8
  446.4 7.3 %copy-start.7 = (bf16[4096]{0:T(1024)(128)(2,1)S(1)}, bf16[4096]{0:T(1024)(128)(2,1)}, u32[]{:S(2)}) copy-start(bf16[4096]{0:T(1024)(128)(2,1)} %param.15) | copy-start | bytes 24580
  450.4 58.8 %collective-permute-start.4 = (f32[64,128,64]{1,2,0:T(8,128)}, f32[64,128,64]{1,2,0:T(8,128)}, u32[]{:S(2)}, u32[]{:S(2)}) collective-permute-start(f32[64,128,64]{1,2,0:T(8,128)} %select_add_fusion.1), channel_id=1, source_target_pairs={{0,8},{2,10},{4,12},{6,14},{8,0},{10,2},{12,4},{14,6},{16,24},{18,... | collective-permute-start | bytes 6291464 | tf_op jit(solution)/shard_map/ppermute | solution.py:8
  452.4 43.0 %collective-permute-start.5 = (f32[64]{0:T(128)S(1)}, f32[64]{0:T(128)S(1)}, u32[]{:S(2)}, u32[]{:S(2)}) collective-permute-start(f32[64]{0:T(128)S(1)} %get-tuple-element.124), channel_id=1, source_target_pairs={{0,8},{2,10},{4,12},{6,14},{8,0},{10,2},{12,4},{14,6},{16,24},{18,... | collective-permute-start | bytes 776 | tf_op jit(solution)/shard_map/ppermute | solution.py:8
  511.7 93.4 %collective-permute-start.6 = (f32[64,128,64]{1,2,0:T(8,128)S(1)}, f32[64,128,64]{1,2,0:T(8,128)S(1)}, u32[]{:S(2)}, u32[]{:S(2)}) collective-permute-start(f32[64,128,64]{1,2,0:T(8,128)S(1)} %select_add_fusion), channel_id=1, source_target_pairs={{0,16},{2,18},{4,20},{6,22},{8,24},{10,26},{12,28},{14,30},{16,0},... | collective-permute-start | bytes 6291464 | tf_op jit(solution)/shard_map/ppermute | solution.py:8
  544.7 67.0 %copy-start.2 = (f32[64,768]{1,0:T(8,128)S(1)}, f32[64,768]{1,0:T(8,128)}, u32[]{:S(2)}) copy-start(f32[64,768]{1,0:T(8,128)} %slice_bitcast_fusion) | copy-start | bytes 589828
  544.7 67.0 %copy-start.3 = (f32[64,768]{1,0:T(8,128)S(1)}, f32[64,768]{1,0:T(8,128)}, u32[]{:S(2)}) copy-start(f32[64,768]{1,0:T(8,128)} %get-tuple-element.120) | copy-start | bytes 589828
  544.7 67.0 %copy-start.4 = (f32[64,768]{1,0:T(8,128)S(1)}, f32[64,768]{1,0:T(8,128)}, u32[]{:S(2)}) copy-start(f32[64,768]{1,0:T(8,128)} %get-tuple-element.121) | copy-start | bytes 589828
  544.7 67.0 %copy-start.5 = (f32[64,768]{1,0:T(8,128)S(1)}, f32[64,768]{1,0:T(8,128)}, u32[]{:S(2)}) copy-start(f32[64,768]{1,0:T(8,128)} %get-tuple-element.122) | copy-start | bytes 589828
  544.7 67.0 %copy-start.6 = (f32[64,768]{1,0:T(8,128)S(1)}, f32[64,768]{1,0:T(8,128)}, u32[]{:S(2)}) copy-start(f32[64,768]{1,0:T(8,128)} %get-tuple-element.123) | copy-start | bytes 589828
  544.7 67.0 %copy-start.8 = (f32[64]{0:T(128)S(1)}, f32[64]{0:T(128)}, u32[]{:S(2)}) copy-start(f32[64]{0:T(128)} %param.14) | copy-start | bytes 772
  676.6 9.0 %copy-start.1 = (bf16[768,128]{1,0:T(8,128)(2,1)S(1)}, bf16[768,128]{1,0:T(8,128)(2,1)}, u32[]{:S(2)}) copy-start(bf16[768,128]{1,0:T(8,128)(2,1)} %param.9) | copy-start | bytes 589828
where the time goes:
time: 693 us; the launch traced here: 686 us
  matrix products  349 us (50%)
  waiting for transfers between devices  192 us (28%)
  other arithmetic  74.5 us (11%)
  local copies, waits for them, and re-layouts  62.4 us (9%)
    ppermute x7, waiting for transfers between devices, partner(): lax.ppermute(value, axis, [(i, i ^ 1 << stride) for i in range(lax.axis_s...  192 us
    dot_general x64, matrix products, head_terms(): inner = jnp.dot(mixing, head_vals, preferred_element_type=jnp.float32)  141 us
    dot_general x64, matrix products, head_terms(): jnp.einsum('sn,sp->np', scaled_keys, head_vals, preferred_element_type=jn...  116 us
    dot_general x4, matrix products, split_project(): jnp.einsum('tn,hnp->htp', queries, upper_part, preferred_element_type=jnp...  61.1 us
    exp x64, other arithmetic, head_terms(): jnp.exp(cum_head[-1] - cum_head)[:, None]  39.7 us
    slice x64, local copies, waits for them, and re-layouts, head_terms(): cum_head[-1] - cum_head  37.8 us
    dot_general x4, matrix products, split_project(): jnp.einsum('tn,hnp->htp', queries, lower_part, preferred_element_type=jnp...  29.7 us
  transfers between devices with their start and end apart: 7, of which 4 were waited for; matrix products, arithmetic and copies ran while one was open for 7% of the time, Pallas kernels for 0%

commit v1 on v0

v1 whole, which is shorter than its diff:
```python
import functools

import jax
import jax.numpy as jnp
from jax import lax
from jax.experimental import pallas as pl
from jax.experimental.pallas import tpu as pltpu
from jax.sharding import PartitionSpec as P

F32 = jnp.float32
BF16 = jnp.bfloat16
SUB = 128
CHUNKS = 4
GROUP = 8


def dot(a, b, dims=((1,), (0,))):
    return lax.dot_general(a, b, (dims, ((), ())), preferred_element_type=F32)


def split3(x):
    hi = x.astype(BF16)
    r = x - hi.astype(F32)
    mid = r.astype(BF16)
    return hi, mid, (r - mid.astype(F32)).astype(BF16)


def factors_kernel(decay_ref, lw_ref, src_ref, dst_ref, tail_ref, grow_ref, fa_ref, fb_ref, tot_ref):
    heads, toks = decay_ref.shape
    row = lax.broadcasted_iota(jnp.int32, (SUB, SUB), 0)
    col = lax.broadcasted_iota(jnp.int32, (SUB, SUB), 1)
    tri = jnp.where(row <= col, 1.0, 0.0).astype(BF16)
    subs = toks // SUB
    base = jnp.zeros((heads, 1), F32)
    local = []
    for i in range(subs):
        at = pl.ds(i * SUB, SUB)
        hi, mid, lo = split3(decay_ref[:, at])
        cum = dot(hi, tri) + dot(mid, tri) + dot(lo, tri)
        middle = cum[:, SUB // 2 - 1 : SUB // 2]
        end = cum[:, SUB - 1 : SUB]
        src_ref[:, at] = jnp.exp(middle - cum)
        dst_ref[:, at] = jnp.exp(cum - middle) * lw_ref[0, :, :][:, i * SUB : (i + 1) * SUB].astype(F32)
        fa_ref[:, at] = jnp.broadcast_to(jnp.exp(end - middle), (heads, SUB))
        fb_ref[:, at] = jnp.broadcast_to(jnp.exp(middle), (heads, SUB))
        full = cum + base
        grow_ref[:, at] = jnp.exp(full)
        local.append(full)
        base = base + end
    for i in range(subs):
        tail_ref[:, pl.ds(i * SUB, SUB)] = jnp.exp(jnp.minimum(base - local[i], 0.0))
    tot_ref[...] = jnp.broadcast_to(base, (heads, SUB))


def make_factors(log_decay, level_weight):
    heads, toks = log_decay.shape
    big = jax.ShapeDtypeStruct((heads, toks), F32)
    return pl.pallas_call(
        factors_kernel,
        out_shape=(big, big, big, big, big, big, jax.ShapeDtypeStruct((heads, SUB), F32)),
        grid=(1,),
        in_specs=[
            pl.BlockSpec((heads, toks), lambda i: (0, 0)),
            pl.BlockSpec((1, heads, toks), lambda i: (0, 0, 0)),
        ],
        out_specs=tuple([pl.BlockSpec((heads, toks), lambda i: (0, 0))] * 6 + [pl.BlockSpec((heads, SUB), lambda i: (0, 0))]),
        name="factors",
    )(log_decay, level_weight)


def scale_heads(x_t, fac, size):
    g = fac.shape[0]
    return (x_t.reshape(g, size, x_t.shape[1]) * fac[:, None, :]).reshape(x_t.shape)


def state_kernel(size, v_ref, k_ref, tail_ref, s_ref):
    v_t = v_ref[...].T.astype(F32)
    scaled = scale_heads(v_t, tail_ref[...], size).astype(BF16)
    s_ref[...] = dot(scaled, k_ref[...])


def chunk_state(values, keys, tail, chunk, chunks, group):
    toks, width = values.shape
    heads = tail.shape[0]
    size = width // heads
    n = keys.shape[1]
    rows = group * size
    steps = heads // chunks // group
    first = chunk * steps
    return pl.pallas_call(
        functools.partial(state_kernel, size),
        out_shape=jax.ShapeDtypeStruct((steps * rows, n), F32),
        grid=(steps,),
        in_specs=[
            pl.BlockSpec((toks, rows), lambda i: (0, first + i)),
            pl.BlockSpec((toks, n), lambda i: (0, 0)),
            pl.BlockSpec((group, toks), lambda i: (first + i, 0)),
        ],
        out_specs=pl.BlockSpec((rows, n), lambda i: (i, 0)),
        cost_estimate=pl.CostEstimate(
            flops=2 * steps * rows * toks * n, bytes_accessed=2 * toks * steps * rows + 4 * steps * rows * n, transcendentals=0
        ),
        name="state",
    )(values, keys, tail)


def mix_kernel(size, levels, *refs):
    (v_ref, q_ref, k_ref, src_ref, dst_ref, fa_ref, fb_ref, coef_ref, skip_ref, gain_ref) = refs[:10]
    bucket_refs = refs[10 : 10 + levels]
    x_ref, sq_ref, qt_ref, mt_ref = refs[-4:]
    toks = v_ref.shape[0]
    rows = v_ref.shape[1]
    subs = toks // SUB
    step = pl.program_id(0)

    @pl.when(step == 0)
    def _():
        qt_ref[...] = q_ref[...].T
        row = lax.broadcasted_iota(jnp.int32, (SUB, SUB), 0)
        col = lax.broadcasted_iota(jnp.int32, (SUB, SUB), 1)
        for i in range(subs):
            at = pl.ds(i * SUB, SUB)
            sc = dot(k_ref[at, :], q_ref[at, :], ((1,), (1,)))
            mt_ref[:, at] = jnp.where(row <= col, sc, 0.0).astype(BF16)
        sq_ref[...] = jnp.zeros_like(sq_ref)

    v_t = v_ref[...].T.astype(F32)
    scaled = scale_heads(v_t, src_ref[...], size).astype(BF16)
    run = None
    inner = []
    for i in range(subs):
        cols = slice(i * SUB, (i + 1) * SUB)
        at = pl.ds(i * SUB, SUB)
        part = dot(scaled[:, cols], mt_ref[:, at])
        if i > 0:
            begin = scale_heads(run, fb_ref[:, at], size)
            part = part + dot(begin.astype(BF16), qt_ref[:, at])
        inner.append(part)
        if i < subs - 1:
            kv = dot(scaled[:, cols], k_ref[at, :])
            run = scale_heads(kv if i == 0 else begin + kv, fa_ref[:, at], size)
    x = scale_heads(jnp.concatenate(inner, axis=1), dst_ref[...], size)
    x = x + scale_heads(v_t, skip_ref[...], size)
    for l in range(levels):
        proj = dot(bucket_refs[l][...].astype(BF16), qt_ref[...])
        x = x + scale_heads(proj, coef_ref[l], size)
    sq = (x * x).reshape(rows // 8, 8, toks).sum(axis=0)
    sq_ref[...] += sq
    x_ref[...] = x * gain_ref[...][:, :1]


def chunk_mix(values, queries, keys, src, dst, fa, fb, coef, skip_b, gain_b, buckets, chunk, chunks, group):
    toks, width = values.shape
    heads = src.shape[0]
    size = width // heads
    n = keys.shape[1]
    rows = group * size
    steps = heads // chunks // group
    first = chunk * steps
    levels = len(buckets)
    whole = pl.BlockSpec((toks, n), lambda i: (0, 0))
    per_head = pl.BlockSpec((group, toks), lambda i: (first + i, 0))
    return pl.pallas_call(
        functools.partial(mix_kernel, size, levels),
        out_shape=(jax.ShapeDtypeStruct((steps * rows, toks), F32), jax.ShapeDtypeStruct((8, toks), F32)),
        grid=(steps,),
        in_specs=[
            pl.BlockSpec((toks, rows), lambda i: (0, first + i)),
            whole,
            whole,
            per_head,
            per_head,
            per_head,
            per_head,
            pl.BlockSpec((levels, group, toks), lambda i: (0, first + i, 0)),
            per_head,
            pl.BlockSpec((rows, SUB), lambda i: (first + i, 0)),
        ]
        + [pl.BlockSpec((rows, n), lambda i: (i, 0))] * levels,
        out_specs=(pl.BlockSpec((rows, toks), lambda i: (i, 0)), pl.BlockSpec((8, toks), lambda i: (0, 0))),
        scratch_shapes=[pltpu.VMEM((n, toks), BF16), pltpu.VMEM((SUB, toks), BF16)],
        cost_estimate=pl.CostEstimate(
            flops=2 * steps * rows * toks * n * (levels + 3), bytes_accessed=6 * toks * steps * rows, transcendentals=0
        ),
        name="mix",
    )(values, queries, keys, src, dst, fa, fb, coef, skip_b, gain_b, *buckets)


def norm_kernel(chunks, steps, inv_ref, *refs):
    x_refs, o_ref = refs[:chunks], refs[chunks]
    step = pl.program_id(0)
    for c in range(chunks):

        @pl.when(step // steps == c)
        def _():
            o_ref[...] = (x_refs[c][...] * inv_ref[...]).astype(BF16).T


def normalize(parts, inv_rms, rows):
    chunks = len(parts)
    chunk_rows, toks = parts[0].shape
    steps = chunk_rows // rows

    def pick(c):
        return lambda i: (jnp.clip(i - c * steps, 0, steps - 1), 0)

    return pl.pallas_call(
        functools.partial(norm_kernel, chunks, steps),
        out_shape=jax.ShapeDtypeStruct((toks, chunks * chunk_rows), BF16),
        grid=(chunks * steps,),
        in_specs=[pl.BlockSpec((1, toks), lambda i: (0, 0))] + [pl.BlockSpec((rows, toks), pick(c)) for c in range(chunks)],
        out_specs=pl.BlockSpec((toks, rows), lambda i: (0, i)),
        name="normalize",
    )(inv_rms, *parts)


def swap(value, axis, stride):
    return lax.ppermute(value, axis, [(i, i ^ (1 << stride)) for i in range(lax.axis_size(axis))])


def raise_up(value, axis, stride):
    half = 1 << stride
    return lax.ppermute(value, axis, [(i, i ^ half) for i in range(lax.axis_size(axis)) if not i & half])


def shards(queries, keys, values, log_decay, level_weight, skip, norm_gain):
    toks, width = values.shape
    heads = log_decay.shape[0]
    size = width // heads
    group = min(GROUP, heads)
    chunks = min(CHUNKS, heads // group)
    chunk_heads = heads // chunks
    levels = lax.axis_size("seq").bit_length() - 1
    index = lax.axis_index("seq")

    src, dst, tail, grow, fa, fb, tot = make_factors(log_decay, level_weight)

    group_total = tot[:, 0]
    offset = jnp.zeros_like(group_total)
    offsets, rights, flags = [], [], []
    for l in range(levels):
        bit = (index >> l) & 1
        other = swap(group_total, "seq", l)
        flags.append(bit == 1)
        offsets.append(jnp.where(bit == 1, jnp.exp(offset), 0.0))
        rights.append(jnp.exp(jnp.where(bit == 1, group_total, other)))
        offset = offset + jnp.where(bit == 1, other, 0.0)
        group_total = group_total + other
    coef = level_weight[1:].astype(F32) * grow[None] * jnp.stack(offsets)[:, :, None]

    skip_b = jnp.broadcast_to(skip[:, None], (heads, toks))
    gain_b = jnp.broadcast_to(norm_gain.astype(F32)[:, None], (width, SUB))

    states = [chunk_state(values, keys, tail, c, chunks, group) for c in range(chunks)]
    parts, squares = [], []
    for c in range(chunks):
        here = slice(c * chunk_heads, (c + 1) * chunk_heads)
        state = states[c]
        buckets = []
        for l in range(levels):
            if l + 1 < levels:
                got = swap(state, "seq", l)
                left = jnp.where(flags[l], got, state)
                right = jnp.where(flags[l], state, got)
                fac = jnp.repeat(rights[l][here], size)[:, None]
                state = fac * left + right
            else:
                got = raise_up(state, "seq", l)
            buckets.append(got)
        part, sq = chunk_mix(
            values, queries, keys, src, dst, fa, fb, coef, skip_b, gain_b, buckets, c, chunks, group
        )
        parts.append(part)
        squares.append(sq)
    sq = functools.reduce(jnp.add, squares).sum(axis=0)
    count = lax.axis_size("head")
    total = sq
    if count == 2:
        total = sq + lax.ppermute(sq, "head", [(0, 1), (1, 0)])
    else:
        total = lax.psum(sq, "head")
    inv_rms = lax.rsqrt(total / (width * count) + 1e-05)
    return normalize(parts, inv_rms[None, :], group * size)


def solution(mesh):
    placed = (
        P("seq", None),
        P("seq", None),
        P("seq", "head"),
        P("head", "seq"),
        P(None, "head", "seq"),
        P("head"),
        P("head"),
    )
    return jax.shard_map(
        shards, mesh=mesh, in_specs=placed, out_specs=P("seq", "head"), check_vma=False
    )
```

time: 693 us -> 208 us (0.30); the launches traced: 686 us -> 208 us
  matrix products: 349 us -> 0 us
  waiting for transfers between devices: 192 us -> 117 us
  other arithmetic: 74.5 us -> 8.51 us
  local copies, waits for them, and re-layouts: 62.4 us -> 7.05 us
  Pallas kernels: 0 us -> 54.1 us
  starting transfers between devices: 4.63 us -> 20.2 us
    dot_general x137 -> x0, matrix products: 349 us -> none  [the longest x64 141 us: head_terms(): inner = jnp.dot(mixing, head_vals, preferred_element_type=jnp.float32)]
    ppermute x7 -> x20, waiting for transfers between devices: 192 us -> 117 us  [the longest x15 73.2 us: swap(): lax.ppermute(value, axis, [(i, i ^ 1 << stride) for i in range(lax.axis_s...]
    pallas_call x0 -> x10, Pallas kernels: none -> 54.1 us  [the longest x4 29.2 us: chunk_mix(): pl.pallas_call(functools.partial(mix_kernel, size, levels), out_shape=(ja...]
    exp x64 -> x3, other arithmetic: 39.7 us -> 0.02 us  [shards(): rights.append(jnp.exp(jnp.where(bit == 1, group_total, other)))]
    slice x66 -> x4, local copies, waits for them, and re-layouts: 38.2 us -> 1.08 us  [the longest x1 0.86 us: shards(): group_total = tot[:, 0]]
    ppermute x7 -> x20, starting transfers between devices: 4.63 us -> 20.2 us  [the longest x15 14.1 us: swap(): lax.ppermute(value, axis, [(i, i ^ 1 << stride) for i in range(lax.axis_s...]
    reshape x2 -> x0, local copies, waits for them, and re-layouts: 13.5 us -> none  [the longest x1 12.6 us: shards(): scaled_out.transpose(1, 0, 2).reshape(tok_rows, chan_width)]
    convert_element_type x4 -> x0, other arithmetic: 11 us -> none  [the longest x1 8.96 us: shards(): return result_rows.astype(jnp.bfloat16)]
  transfers between devices with their start and end apart: 7 -> 20, of which waited for: 4 -> 12; matrix products, arithmetic and copies ran while one was open for 7% -> 6% of each run, Pallas kernels for 0% -> 16%
where the time goes in v1:
time: 208 us
  waiting for transfers between devices  117 us (56%)
  Pallas kernels  54.1 us (26%)
  starting transfers between devices  20.2 us (10%)
  other arithmetic  8.51 us (4%)
  local copies, waits for them, and re-layouts  7.05 us (3%)
    ppermute x15, waiting for transfers between devices, swap(): lax.ppermute(value, axis, [(i, i ^ 1 << stride) for i in range(lax.axis_s...  73.2 us
    ppermute x4, waiting for transfers between devices, raise_up(): lax.ppermute(value, axis, [(i, i ^ half) for i in range(lax.axis_size(axi...  43.3 us
    pallas_call x4, Pallas kernels, chunk_mix(): pl.pallas_call(functools.partial(mix_kernel, size, levels), out_shape=(ja...  29.2 us
    ppermute x15, starting transfers between devices, swap(): lax.ppermute(value, axis, [(i, i ^ 1 << stride) for i in range(lax.axis_s...  14.1 us
    pallas_call x1, Pallas kernels, normalize(): pl.pallas_call(functools.partial(norm_kernel, chunks, steps), out_shape=j...  11.3 us
    pallas_call x4, Pallas kernels, chunk_state(): pl.pallas_call(functools.partial(state_kernel, size), out_shape=jax.Shape...  11 us
    add x12, other arithmetic, shards(): state = fac * left + right  6.65 us
    ppermute x4, starting transfers between devices, raise_up(): lax.ppermute(value, axis, [(i, i ^ half) for i in range(lax.axis_size(axi...  5.46 us
  transfers between devices with their start and end apart: 20, of which 12 were waited for; matrix products, arithmetic and copies ran while one was open for 6% of the time, Pallas kernels for 16%

profile of v1, /device:TPU:25, one launch (start us, length us, event | category | flops | bytes accessed | tf_op | source)
XLA Modules:
  0.0 207.5 jit_solution(14933388954585554704)
XLA Ops:
  0.0 2.5 %factors.1 = (f32[64,768]{1,0:T(8,128)}, f32[64,768]{1,0:T(8,128)}, f32[64,768]{1,0:T(8,128)}, f32[64,768]{1,0:T(8,128)}, f32[64,768]{1,0:T(8,128)}, /*index=5*/f32[64,768]{1,0:T(8,128)}, f32[64,128]{1,0:T(8,128)}) custom-call(f32[64,768]{1,0:T(8,128)} %decay_ref.1, bf16[5,64,768]{2,1,0:T(8,128)(2,1)} %lw_ref.1), custom_call_target="tpu_custom_call" | custom-call | tf_op jit(solution)/shard_map/factors/pallas_call | solution.py:58
  2.5 0.9 slice_reduce_fusion
  3.4 1.3 collective-permute-start
  4.6 2.7 %state.4 = f32[1024,128]{1,0:T(8,128)} custom-call(bf16[768,4096]{1,0:T(8,128)(2,1)} %refs_0_.7, bf16[768,128]{1,0:T(8,128)(2,1)} %refs_2_.7, f32[64,768]{1,0:T(8,128)} %get-tuple-element.26.tail_ref), custom_call_target="tpu_custom_call" | custom-call | flops 201326592 | bytes 2097152 | tf_op jit(solution)/shard_map/state/pallas_call | solution.py:90
  7.6 2.8 %state.5 = f32[1024,128]{1,0:T(8,128)} custom-call(bf16[768,4096]{1,0:T(8,128)(2,1)} %refs_0_.7, bf16[768,128]{1,0:T(8,128)(2,1)} %refs_2_.7, f32[64,768]{1,0:T(8,128)} %get-tuple-element.26.tail_ref), custom_call_target="tpu_custom_call" | custom-call | flops 201326592 | bytes 2097152 | tf_op jit(solution)/shard_map/state/pallas_call | solution.py:90
  10.4 1.2 collective-permute-start.7
  11.6 2.8 %state.6 = f32[1024,128]{1,0:T(8,128)} custom-call(bf16[768,4096]{1,0:T(8,128)(2,1)} %refs_0_.7, bf16[768,128]{1,0:T(8,128)(2,1)} %refs_2_.7, f32[64,768]{1,0:T(8,128)} %get-tuple-element.26.tail_ref), custom_call_target="tpu_custom_call" | custom-call | flops 201326592 | bytes 2097152 | tf_op jit(solution)/shard_map/state/pallas_call | solution.py:90
  14.6 2.8 %state.7 = f32[1024,128]{1,0:T(8,128)} custom-call(bf16[768,4096]{1,0:T(8,128)(2,1)} %refs_0_.7, bf16[768,128]{1,0:T(8,128)(2,1)} %refs_2_.7, f32[64,768]{1,0:T(8,128)} %get-tuple-element.26.tail_ref), custom_call_target="tpu_custom_call" | custom-call | flops 201326592 | bytes 2097152 | tf_op jit(solution)/shard_map/state/pallas_call | solution.py:90
  17.4 1.2 collective-permute-start.15
  19.0 1.3 collective-permute-start.1
  20.5 1.2 collective-permute-done.1
  22.6 2.3 %collective-permute-done.2 = f32[64]{0:T(128)S(1)} collective-permute-done((f32[64]{0:T(128)S(1)}, f32[64]{0:T(128)S(1)}, u32[]{:S(2)}, u32[]{:S(2)}) %collective-permute-start.2) | collective-permute-done | bytes 288 | tf_op jit(solution)/shard_map/ppermute | solution.py:218
  25.6 1.4 select_add_fusion.11
  27.0 1.3 collective-permute-start.4
  28.3 3.0 %collective-permute-done.7.refs_10_ = f32[1024,128]{1,0:T(8,128)S(1)} collective-permute-done((f32[1024,128]{1,0:T(8,128)}, f32[1024,128]{1,0:T(8,128)S(1)}, u32[]{:S(2)}, u32[]{:S(2)}) %collective-permute-start.7) | collective-permute-done | bytes 524320 | tf_op jit(solution)/shard_map/ppermute | solution.py:218
  31.4 1.4 select_add_fusion.8
  32.8 1.3 collective-permute-start.8
  34.1 8.5 %collective-permute-done.11.refs_10_ = f32[1024,128]{1,0:T(8,128)S(1)} collective-permute-done((f32[1024,128]{1,0:T(8,128)}, f32[1024,128]{1,0:T(8,128)S(1)}, u32[]{:S(2)}, u32[]{:S(2)}) %collective-permute-start.11) | collective-permute-done | bytes 524320 | tf_op jit(solution)/shard_map/ppermute | solution.py:218
  42.8 1.3 collective-permute-start.12
  44.1 9.7 %collective-permute-done.15.refs_10_ = f32[1024,128]{1,0:T(8,128)S(1)} collective-permute-done((f32[1024,128]{1,0:T(8,128)}, f32[1024,128]{1,0:T(8,128)S(1)}, u32[]{:S(2)}, u32[]{:S(2)}) %collective-permute-start.15) | collective-permute-done | bytes 524320 | tf_op jit(solution)/shard_map/ppermute | solution.py:218
  54.1 1.3 collective-permute-start.16
  56.1 1.4 collective-permute-start.9
  57.5 13.0 %collective-permute-done.16.refs_11_ = f32[1024,128]{1,0:T(8,128)S(1)} collective-permute-done((f32[1024,128]{1,0:T(8,128)S(1)}, f32[1024,128]{1,0:T(8,128)S(1)}, u32[]{:S(2)}, u32[]{:S(2)}) %collective-permute-start.16) | collective-permute-done | bytes 524320 | tf_op jit(solution)/shard_map/ppermute | solution.py:218
  71.2 1.3 collective-permute-start.13
  72.5 5.8 %collective-permute-done.9.refs_12_ = f32[1024,128]{1,0:T(8,128)S(1)} collective-permute-done((f32[1024,128]{1,0:T(8,128)S(1)}, f32[1024,128]{1,0:T(8,128)S(1)}, u32[]{:S(2)}, u32[]{:S(2)}) %collective-permute-start.9) | collective-permute-done | bytes 524320 | tf_op jit(solution)/shard_map/ppermute | solution.py:218
  78.3 1.0 select_add_fusion.6
  79.4 1.4 collective-permute-start.10
  80.8 20.0 %collective-permute-done.17.refs_12_ = f32[1024,128]{1,0:T(8,128)S(1)} collective-permute-done((f32[1024,128]{1,0:T(8,128)S(1)}, f32[1024,128]{1,0:T(8,128)S(1)}, u32[]{:S(2)}, u32[]{:S(2)}) %collective-permute-start.17) | collective-permute-done | bytes 524320 | tf_op jit(solution)/shard_map/ppermute | solution.py:218
  101.0 1.3 collective-permute-start.18
  102.3 9.8 %collective-permute-done.13.refs_12_ = f32[1024,128]{1,0:T(8,128)S(1)} collective-permute-done((f32[1024,128]{1,0:T(8,128)S(1)}, f32[1024,128]{1,0:T(8,128)S(1)}, u32[]{:S(2)}, u32[]{:S(2)}) %collective-permute-start.13) | collective-permute-done | bytes 524320 | tf_op jit(solution)/shard_map/ppermute | solution.py:218
  112.1 1.0 select_add_fusion.3
  113.1 1.3 collective-permute-start.14
  114.7 1.5 collective-permute-start.6
  116.2 1.0 multiply_multiply_fusion.refs_7_
  117.2 42.0 %collective-permute-done.18.refs_13_ = f32[1024,128]{1,0:T(8,128)S(1)} collective-permute-done((f32[1024,128]{1,0:T(8,128)S(1)}, f32[1024,128]{1,0:T(8,128)S(1)}, u32[]{:S(2)}, u32[]{:S(2)}) %collective-permute-start.18) | collective-permute-done | bytes 524320 | tf_op jit(solution)/shard_map/ppermute | solution.py:223
  159.2 0.9 broadcast_in_dim.64.refs_8_
  160.1 1.9 broadcast_in_dim.65.refs_9_
  162.0 7.2 %mix.7 = (f32[1024,768]{1,0:T(8,128)}, f32[8,768]{1,0:T(8,128)}) custom-call(bf16[768,4096]{1,0:T(8,128)(2,1)} %refs_0_.7, bf16[768,128]{1,0:T(8,128)(2,1)} %refs_1_.7, bf16[768,128]{1,0:T(8,128)(2,1)} %refs_2_.7, f32[64,768]{1,0:T(8,128)} %get-tuple-element.20.refs_3_, f32[64,768]{1,0:T(8,128)} %get-tuple-element.21.refs_4_, ...), custom_call_target="tpu_custom_call" | custom-call | flops 1409286144 | bytes 4718592 | tf_op jit(solution)/shard_map/mix/pallas_call | solution.py:163
  169.2 1.3 collective-permute-done.14.refs_13_
  170.5 7.3 %mix.6 = (f32[1024,768]{1,0:T(8,128)}, f32[8,768]{1,0:T(8,128)}) custom-call(bf16[768,4096]{1,0:T(8,128)(2,1)} %refs_0_.7, bf16[768,128]{1,0:T(8,128)(2,1)} %refs_1_.7, bf16[768,128]{1,0:T(8,128)(2,1)} %refs_2_.7, f32[64,768]{1,0:T(8,128)} %get-tuple-element.20.refs_3_, f32[64,768]{1,0:T(8,128)} %get-tuple-element.21.refs_4_, ...), custom_call_target="tpu_custom_call" | custom-call | flops 1409286144 | bytes 4718592 | tf_op jit(solution)/shard_map/mix/pallas_call | solution.py:163
  177.8 7.3 %mix.5 = (f32[1024,768]{1,0:T(8,128)}, f32[8,768]{1,0:T(8,128)}) custom-call(bf16[768,4096]{1,0:T(8,128)(2,1)} %refs_0_.7, bf16[768,128]{1,0:T(8,128)(2,1)} %refs_1_.7, bf16[768,128]{1,0:T(8,128)(2,1)} %refs_2_.7, f32[64,768]{1,0:T(8,128)} %get-tuple-element.20.refs_3_, f32[64,768]{1,0:T(8,128)} %get-tuple-element.21.refs_4_, ...), custom_call_target="tpu_custom_call" | custom-call | flops 1409286144 | bytes 4718592 | tf_op jit(solution)/shard_map/mix/pallas_call | solution.py:163
  185.2 0.8 copy-done.15
  186.0 7.3 %mix.4 = (f32[1024,768]{1,0:T(8,128)}, f32[8,768]{1,0:T(8,128)}) custom-call(bf16[768,4096]{1,0:T(8,128)(2,1)} %refs_0_.7, bf16[768,128]{1,0:T(8,128)(2,1)} %refs_1_.7, bf16[768,128]{1,0:T(8,128)(2,1)} %refs_2_.7, f32[64,768]{1,0:T(8,128)} %get-tuple-element.20.refs_3_, f32[64,768]{1,0:T(8,128)} %get-tuple-element.21.refs_4_, ...), custom_call_target="tpu_custom_call" | custom-call | flops 1409286144 | bytes 4718592 | tf_op jit(solution)/shard_map/mix/pallas_call | solution.py:163
  193.3 0.8 add_reduce_fusion
  194.1 0.7 collective-permute-start.19
  194.8 0.8 collective-permute-done.19
  195.6 0.6 broadcast_in_dim.78.inv_ref
  196.2 11.3 %normalize.1 = bf16[768,4096]{1,0:T(8,128)(2,1)} custom-call(f32[1,768]{1,0:T(1,128)} %broadcast_in_dim.78.inv_ref, f32[1024,768]{1,0:T(8,128)} %get-tuple-element.31.refs_0_, f32[1024,768]{1,0:T(8,128)} %get-tuple-element.32.refs_1_, f32[1024,768]{1,0:T(8,128)} %get-tuple-element.33.refs_2_, f32[1024,768]{1,0:T(8,128)} %get-tuple-element.34.refs_3_), custom_call_target="tpu_custom_call" | custom-call | tf_op jit(solution)/shard_map/normalize/pallas_call | solution.py:207
  (99 shorter events, 5.1 us)
Async XLA Ops:
  3.4 15.3 %collective-permute-start = (f32[64]{0:T(128)S(1)}, f32[64]{0:T(128)S(1)}, u32[]{:S(2)}, u32[]{:S(2)}) collective-permute-start(f32[64]{0:T(128)S(1)} %slice_reduce_fusion), channel_id=1, source_target_pairs={{0,2},{2,0},{4,6},{6,4},{8,10},{10,8},{12,14},{14,12},{16,18},{18,... | collective-permute-start | bytes 776 | tf_op jit(solution)/shard_map/ppermute | solution.py:218
  7.4 18.2 %collective-permute-start.3 = (f32[1024,128]{1,0:T(8,128)}, f32[1024,128]{1,0:T(8,128)S(1)}, u32[]{:S(2)}, u32[]{:S(2)}) collective-permute-start(f32[1024,128]{1,0:T(8,128)} %state.4), channel_id=1, source_target_pairs={{0,2},{2,0},{4,6},{6,4},{8,10},{10,8},{12,14},{14,12},{16,18},{18,... | collective-permute-start | bytes 1572872 | tf_op jit(solution)/shard_map/ppermute | solution.py:218
  10.4 20.9 %collective-permute-start.7 = (f32[1024,128]{1,0:T(8,128)}, f32[1024,128]{1,0:T(8,128)S(1)}, u32[]{:S(2)}, u32[]{:S(2)}) collective-permute-start(f32[1024,128]{1,0:T(8,128)} %state.5), channel_id=1, source_target_pairs={{0,2},{2,0},{4,6},{6,4},{8,10},{10,8},{12,14},{14,12},{16,18},{18,... | collective-permute-start | bytes 1572872 | tf_op jit(solution)/shard_map/ppermute | solution.py:218
  14.4 28.2 %collective-permute-start.11 = (f32[1024,128]{1,0:T(8,128)}, f32[1024,128]{1,0:T(8,128)S(1)}, u32[]{:S(2)}, u32[]{:S(2)}) collective-permute-start(f32[1024,128]{1,0:T(8,128)} %state.6), channel_id=1, source_target_pairs={{0,2},{2,0},{4,6},{6,4},{8,10},{10,8},{12,14},{14,12},{16,18},{18,... | collective-permute-start | bytes 1572872 | tf_op jit(solution)/shard_map/ppermute | solution.py:218
  17.4 25.2 %copy-start.5 = (f32[1024,128]{1,0:T(8,128)S(1)}, f32[1024,128]{1,0:T(8,128)}, u32[]{:S(2)}) copy-start(f32[1024,128]{1,0:T(8,128)} %state.6) | copy-start | bytes 1572868
  17.4 36.4 %copy-start.4 = (f32[1024,128]{1,0:T(8,128)S(1)}, f32[1024,128]{1,0:T(8,128)}, u32[]{:S(2)}) copy-start(f32[1024,128]{1,0:T(8,128)} %state.7) | copy-start | bytes 1572868
  17.4 36.4 %collective-permute-start.15 = (f32[1024,128]{1,0:T(8,128)}, f32[1024,128]{1,0:T(8,128)S(1)}, u32[]{:S(2)}, u32[]{:S(2)}) collective-permute-start(f32[1024,128]{1,0:T(8,128)} %state.7), channel_id=1, source_target_pairs={{0,2},{2,0},{4,6},{6,4},{8,10},{10,8},{12,14},{14,12},{16,18},{18,... | collective-permute-start | bytes 1572872 | tf_op jit(solution)/shard_map/ppermute | solution.py:218
  19.0 2.7 %collective-permute-start.1 = (f32[64]{0:T(128)S(1)}, f32[64]{0:T(128)S(1)}, u32[]{:S(2)}, u32[]{:S(2)}) collective-permute-start(f32[64]{0:T(128)S(1)} %get-tuple-element.40), channel_id=1, source_target_pairs={{0,4},{2,6},{4,0},{6,2},{8,12},{10,14},{12,8},{14,10},{16,20},{18,... | collective-permute-start | bytes 776 | tf_op jit(solution)/shard_map/ppermute | solution.py:218
  22.1 2.7 %collective-permute-start.2 = (f32[64]{0:T(128)S(1)}, f32[64]{0:T(128)S(1)}, u32[]{:S(2)}, u32[]{:S(2)}) collective-permute-start(f32[64]{0:T(128)S(1)} %get-tuple-element.38), channel_id=1, source_target_pairs={{0,8},{2,10},{4,12},{6,14},{8,0},{10,2},{12,4},{14,6},{16,24},{18,... | collective-permute-start | bytes 776 | tf_op jit(solution)/shard_map/ppermute | solution.py:218
  25.6 28.5 %copy-start = (f32[1024,128]{1,0:T(8,128)}, f32[1024,128]{1,0:T(8,128)S(1)}, u32[]{:S(2)}) copy-start(f32[1024,128]{1,0:T(8,128)S(1)} %collective-permute-done.3.refs_10_) | copy-start | bytes 1572868
  27.0 28.4 %collective-permute-start.4 = (f32[1024,128]{1,0:T(8,128)S(1)}, f32[1024,128]{1,0:T(8,128)S(1)}, u32[]{:S(2)}, u32[]{:S(2)}) collective-permute-start(f32[1024,128]{1,0:T(8,128)S(1)} %select_add_fusion.11), channel_id=1, source_target_pairs={{0,4},{2,6},{4,0},{6,2},{8,12},{10,14},{12,8},{14,10},{16,20},{18,... | collective-permute-start | bytes 1572872 | tf_op jit(solution)/shard_map/ppermute | solution.py:218
  31.4 24.3 %copy-start.1 = (f32[1024,128]{1,0:T(8,128)}, f32[1024,128]{1,0:T(8,128)S(1)}, u32[]{:S(2)}) copy-start(f32[1024,128]{1,0:T(8,128)S(1)} %collective-permute-done.7.refs_10_) | copy-start | bytes 1572868
  32.8 23.1 %collective-permute-start.8 = (f32[1024,128]{1,0:T(8,128)S(1)}, f32[1024,128]{1,0:T(8,128)S(1)}, u32[]{:S(2)}, u32[]{:S(2)}) collective-permute-start(f32[1024,128]{1,0:T(8,128)S(1)} %select_add_fusion.8), channel_id=1, source_target_pairs={{0,4},{2,6},{4,0},{6,2},{8,12},{10,14},{12,8},{14,10},{16,20},{18,... | collective-permute-start | bytes 1572872 | tf_op jit(solution)/shard_map/ppermute | solution.py:218
  42.6 13.5 %copy-start.2 = (f32[1024,128]{1,0:T(8,128)}, f32[1024,128]{1,0:T(8,128)S(1)}, u32[]{:S(2)}) copy-start(f32[1024,128]{1,0:T(8,128)S(1)} %collective-permute-done.11.refs_10_) | copy-start | bytes 1572868
  42.8 28.1 %collective-permute-start.12 = (f32[1024,128]{1,0:T(8,128)S(1)}, f32[1024,128]{1,0:T(8,128)S(1)}, u32[]{:S(2)}, u32[]{:S(2)}) collective-permute-start(f32[1024,128]{1,0:T(8,128)S(1)} %select_add_fusion.5), channel_id=1, source_target_pairs={{0,4},{2,6},{4,0},{6,2},{8,12},{10,14},{12,8},{14,10},{16,20},{18,... | collective-permute-start | bytes 1572872 | tf_op jit(solution)/shard_map/ppermute | solution.py:218
  53.8 16.9 %copy-start.3 = (f32[1024,128]{1,0:T(8,128)}, f32[1024,128]{1,0:T(8,128)S(1)}, u32[]{:S(2)}) copy-start(f32[1024,128]{1,0:T(8,128)S(1)} %collective-permute-done.15.refs_10_) | copy-start | bytes 1572868
  54.1 16.4 %collective-permute-start.16 = (f32[1024,128]{1,0:T(8,128)S(1)}, f32[1024,128]{1,0:T(8,128)S(1)}, u32[]{:S(2)}, u32[]{:S(2)}) collective-permute-start(f32[1024,128]{1,0:T(8,128)S(1)} %select_add_fusion.2), channel_id=1, source_target_pairs={{0,4},{2,6},{4,0},{6,2},{8,12},{10,14},{12,8},{14,10},{16,20},{18,... | collective-permute-start | bytes 1572872 | tf_op jit(solution)/shard_map/ppermute | solution.py:218
  55.4 15.8 %copy-start.6 = (f32[1024,128]{1,0:T(8,128)}, f32[1024,128]{1,0:T(8,128)S(1)}, u32[]{:S(2)}) copy-start(f32[1024,128]{1,0:T(8,128)S(1)} %collective-permute-done.4.refs_11_) | copy-start | bytes 1572868
  55.6 58.8 %collective-permute-start.5 = (f32[1024,128]{1,0:T(8,128)S(1)}, f32[1024,128]{1,0:T(8,128)S(1)}, u32[]{:S(2)}, u32[]{:S(2)}) collective-permute-start(f32[1024,128]{1,0:T(8,128)S(1)} %select_add_fusion.10), channel_id=1, source_target_pairs={{0,8},{2,10},{4,12},{6,14},{8,0},{10,2},{12,4},{14,6},{16,24},{18,... | collective-permute-start | bytes 1572872 | tf_op jit(solution)/shard_map/ppermute | solution.py:218
  55.9 23.5 %copy-start.7 = (f32[1024,128]{1,0:T(8,128)}, f32[1024,128]{1,0:T(8,128)S(1)}, u32[]{:S(2)}) copy-start(f32[1024,128]{1,0:T(8,128)S(1)} %collective-permute-done.8.refs_11_) | copy-start | bytes 1572868
  56.1 22.2 %collective-permute-start.9 = (f32[1024,128]{1,0:T(8,128)S(1)}, f32[1024,128]{1,0:T(8,128)S(1)}, u32[]{:S(2)}, u32[]{:S(2)}) collective-permute-start(f32[1024,128]{1,0:T(8,128)S(1)} %select_add_fusion.7), channel_id=1, source_target_pairs={{0,8},{2,10},{4,12},{6,14},{8,0},{10,2},{12,4},{14,6},{16,24},{18,... | collective-permute-start | bytes 1572872 | tf_op jit(solution)/shard_map/ppermute | solution.py:218
  70.5 30.5 %copy-start.11 = (f32[1024,128]{1,0:T(8,128)}, f32[1024,128]{1,0:T(8,128)S(1)}, u32[]{:S(2)}) copy-start(f32[1024,128]{1,0:T(8,128)S(1)} %collective-permute-done.16.refs_11_) | copy-start | bytes 1572868
  70.7 30.1 %collective-permute-start.17 = (f32[1024,128]{1,0:T(8,128)S(1)}, f32[1024,128]{1,0:T(8,128)S(1)}, u32[]{:S(2)}, u32[]{:S(2)}) collective-permute-start(f32[1024,128]{1,0:T(8,128)S(1)} %select_add_fusion.1), channel_id=1, source_target_pairs={{0,8},{2,10},{4,12},{6,14},{8,0},{10,2},{12,4},{14,6},{16,24},{18,... | collective-permute-start | bytes 1572872 | tf_op jit(solution)/shard_map/ppermute | solution.py:218
  71.0 42.2 %copy-start.9 = (f32[1024,128]{1,0:T(8,128)}, f32[1024,128]{1,0:T(8,128)S(1)}, u32[]{:S(2)}) copy-start(f32[1024,128]{1,0:T(8,128)S(1)} %collective-permute-done.12.refs_11_) | copy-start | bytes 1572868
  71.2 45.0 %copy-start.14 = (bf16[5,64,768]{2,1,0:T(8,128)(2,1)S(1)}, bf16[5,64,768]{2,1,0:T(8,128)(2,1)}, u32[]{:S(2)}) copy-start(bf16[5,64,768]{2,1,0:T(8,128)(2,1)} %lw_ref.1) | copy-start | bytes 1474564
  71.2 45.0 %copy-start.17 = (f32[64,768]{1,0:T(8,128)S(1)}, f32[64,768]{1,0:T(8,128)}, u32[]{:S(2)}) copy-start(f32[64,768]{1,0:T(8,128)} %get-tuple-element.24) | copy-start | bytes 589828
  71.2 40.9 %collective-permute-start.13 = (f32[1024,128]{1,0:T(8,128)S(1)}, f32[1024,128]{1,0:T(8,128)S(1)}, u32[]{:S(2)}, u32[]{:S(2)}) collective-permute-start(f32[1024,128]{1,0:T(8,128)S(1)} %select_add_fusion.4), channel_id=1, source_target_pairs={{0,8},{2,10},{4,12},{6,14},{8,0},{10,2},{12,4},{14,6},{16,24},{18,... | collective-permute-start | bytes 1572872 | tf_op jit(solution)/shard_map/ppermute | solution.py:218
  78.3 36.4 %copy-start.10 = (f32[1024,128]{1,0:T(8,128)}, f32[1024,128]{1,0:T(8,128)S(1)}, u32[]{:S(2)}) copy-start(f32[1024,128]{1,0:T(8,128)S(1)} %collective-permute-done.9.refs_12_) | copy-start | bytes 1572868
  79.4 79.8 %copy-start.22 = (f32[64]{0:T(128)S(1)}, f32[64]{0:T(128)}, u32[]{:S(2)}) copy-start(f32[64]{0:T(128)} %param.12) | copy-start | bytes 772
  79.4 80.7 %copy-start.21 = (bf16[4096]{0:T(1024)(128)(2,1)S(1)}, bf16[4096]{0:T(1024)(128)(2,1)}, u32[]{:S(2)}) copy-start(bf16[4096]{0:T(1024)(128)(2,1)} %param.13) | copy-start | bytes 24580
  79.4 98.5 %collective-permute-start.10 = (f32[1024,128]{1,0:T(8,128)}, f32[1024,128]{1,0:T(8,128)}, u32[]{:S(2)}, u32[]{:S(2)}) collective-permute-start(f32[1024,128]{1,0:T(8,128)} %select_add_fusion.6), channel_id=1, source_target_pairs={{0,16},{2,18},{4,20},{6,22},{8,24},{10,26},{12,28},{14,30},{1,17},... | collective-permute-start | bytes 1572872 | tf_op jit(solution)/shard_map/ppermute | solution.py:223
  100.8 59.3 %copy-start.12 = (f32[1024,128]{1,0:T(8,128)}, f32[1024,128]{1,0:T(8,128)S(1)}, u32[]{:S(2)}) copy-start(f32[1024,128]{1,0:T(8,128)S(1)} %collective-permute-done.17.refs_12_) | copy-start | bytes 1572868
  101.0 58.2 %collective-permute-start.18 = (f32[1024,128]{1,0:T(8,128)S(1)}, f32[1024,128]{1,0:T(8,128)S(1)}, u32[]{:S(2)}, u32[]{:S(2)}) collective-permute-start(f32[1024,128]{1,0:T(8,128)S(1)} %select_add_fusion), channel_id=1, source_target_pairs={{0,16},{2,18},{4,20},{6,22},{8,24},{10,26},{12,28},{14,30},{1,17},... | collective-permute-start | bytes 1572872 | tf_op jit(solution)/shard_map/ppermute | solution.py:223
  112.1 49.9 %copy-start.13 = (f32[1024,128]{1,0:T(8,128)}, f32[1024,128]{1,0:T(8,128)S(1)}, u32[]{:S(2)}) copy-start(f32[1024,128]{1,0:T(8,128)S(1)} %collective-permute-done.13.refs_12_) | copy-start | bytes 1572868
  113.1 57.4 %collective-permute-start.14 = (f32[1024,128]{1,0:T(8,128)}, f32[1024,128]{1,0:T(8,128)}, u32[]{:S(2)}, u32[]{:S(2)}) collective-permute-start(f32[1024,128]{1,0:T(8,128)} %select_add_fusion.3), channel_id=1, source_target_pairs={{0,16},{2,18},{4,20},{6,22},{8,24},{10,26},{12,28},{14,30},{1,17},... | collective-permute-start | bytes 1572872 | tf_op jit(solution)/shard_map/ppermute | solution.py:223
  114.4 54.8 %copy-start.8 = (f32[1024,128]{1,0:T(8,128)}, f32[1024,128]{1,0:T(8,128)S(1)}, u32[]{:S(2)}) copy-start(f32[1024,128]{1,0:T(8,128)S(1)} %collective-permute-done.5.refs_12_) | copy-start | bytes 1572868
  114.7 70.5 %collective-permute-start.6 = (f32[1024,128]{1,0:T(8,128)S(1)}, f32[1024,128]{1,0:T(8,128)S(1)}, u32[]{:S(2)}, u32[]{:S(2)}) collective-permute-start(f32[1024,128]{1,0:T(8,128)S(1)} %select_add_fusion.9), channel_id=1, source_target_pairs={{0,16},{2,18},{4,20},{6,22},{8,24},{10,26},{12,28},{14,30},{1,17},... | collective-permute-start | bytes 1572872 | tf_op jit(solution)/shard_map/ppermute | solution.py:223
  159.2 0.9 copy-start.16
  185.1 8.2 %copy-start.18 = (f32[8,768]{1,0:T(8,128)S(1)}, f32[8,768]{1,0:T(8,128)}, u32[]{:S(2)}) copy-start(f32[8,768]{1,0:T(8,128)} %get-tuple-element.30) | copy-start | bytes 73732
  185.2 8.2 %copy-start.19 = (f32[8,768]{1,0:T(8,128)S(1)}, f32[8,768]{1,0:T(8,128)}, u32[]{:S(2)}) copy-start(f32[8,768]{1,0:T(8,128)} %get-tuple-element.29) | copy-start | bytes 73732
  185.2 8.2 %copy-start.20 = (f32[8,768]{1,0:T(8,128)S(1)}, f32[8,768]{1,0:T(8,128)}, u32[]{:S(2)}) copy-start(f32[8,768]{1,0:T(8,128)} %get-tuple-element.28) | copy-start | bytes 73732
  185.2 0.8 copy-start.15
  194.1 1.5 collective-permute-start.19
